TPU v7x, 32 devices: a whole 2x2x4 slice. The times are simulated.
32 devices in a mesh: dp: 4 (over y, core), tensor: 8 (over z, x).
Axes of the slice: x: 2, y: 2, z: 4, core: 2. Of those that a mesh axis runs over, the one named last changes fastest.
Arguments:
- hidden_in: bfloat16 [3072, 2048], P(('dp', 'tensor')), may hold values from -6 to 6
- norm1_gain: bfloat16 [2048], replicated, may hold values from 0.099609375 to 1.8984375
- norm2_gain: bfloat16 [2048], replicated, may hold values from 0.099609375 to 1.8984375
- w_query: bfloat16 [2048, 2048], P(None, 'tensor'), may hold values from -0.125 to 0.125
- w_keyval: bfloat16 [2048, 256], replicated, may hold values from -0.125 to 0.125
- w_out: bfloat16 [2048, 2048], P('tensor'), may hold values from -0.5 to 0.5
- w_fc: bfloat16 [2048, 8192], P(None, 'tensor'), may hold values from -0.125 to 0.125
- w_proj: bfloat16 [8192, 2048], P('tensor'), may hold values from -0.0625 to 0.0625
- prefix_kv: bfloat16 [4, 4096, 256], P('dp', 'tensor'), may hold values from -320 to 320
- owner_ids: int32 [4], replicated, may hold values from 0 to 3, each once
- segment_ids: int32 [4, 768], P('dp'), may hold values from 0 to 11, never falling along the last dimension, each value on 1 to 192 neighbouring positions
Outputs:
- layer_out: bfloat16 [3072, 2048], P(('dp', 'tensor'))
- attended: bfloat16 [3072, 2048], P(('dp', 'tensor'))
Inputs may be any that keep to these rules, and one draw needn't show every extreme that they name: `owner_ids`: each stored prefix is extended by exactly one group. `segment_ids`: within a group the request ids never fall; every one of the 12 requests has 1 to 192 tokens, and at least one has exactly 192.
All inputs are finite; a program needn't handle non-finite values.
Results may differ from a plain program's by a relative error of at most 0.015.
Values may be sent and summed in bfloat16 or wider, within the bound.
A program may use at most 128 MiB of HBM per device.

v0:
```python
import math
import jax
import jax.numpy as jnp
from jax import lax
from jax.sharding import PartitionSpec as P


def layer_norm(values, scales):
    widened = values.astype(jnp.float32)
    centre = jnp.mean(widened, axis=-1, keepdims=True)
    centred = widened - centre
    variance = jnp.mean(centred * centred, axis=-1, keepdims=True)
    return (centred * lax.rsqrt(variance + 1e-05) * scales.astype(jnp.float32)).astype(jnp.bfloat16)


def attend_block(state_in, queries, key_rows, value_rows, allowed):
    running, totals, weighted = state_in
    scores = jnp.einsum("htd,kd->htk", queries, key_rows, preferred_element_type=jnp.float32)
    if allowed is not None:
        scores = jnp.where(allowed[None], scores, -jnp.inf)
    new_top = jnp.maximum(running, jnp.max(scores, axis=-1))
    factor = jnp.exp(running - new_top)
    probs = jnp.exp(scores - new_top[..., None])
    totals = totals * factor + jnp.sum(probs, axis=-1)
    probs_b = probs.astype(jnp.bfloat16)
    weighted = weighted * factor[..., None] + jnp.einsum(
        "htk,kd->htd", probs_b, value_rows, preferred_element_type=jnp.float32
    )
    return (new_top, totals, weighted)


def local(
    hidden_in,
    norm1_gain,
    norm2_gain,
    w_query,
    w_keyval,
    w_out,
    w_fc,
    w_proj,
    prefix_kv,
    owner_ids,
    segment_ids,
):
    head_size = w_keyval.shape[1] // 2
    query_cols = w_query.shape[1]
    heads_here = query_cols // head_size
    row_len = segment_ids.shape[1]
    q_scale = 1.0 / math.sqrt(head_size)
    w_joint = jnp.concatenate([w_query, w_keyval], axis=1)
    col_scale = jnp.concatenate(
        [jnp.full((query_cols,), q_scale, jnp.float32), jnp.ones((2 * head_size,), jnp.float32)]
    )
    normed = layer_norm(hidden_in, norm1_gain)
    projected = (
        jnp.dot(
            lax.all_gather(normed, "tensor", axis=0, tiled=True),
            w_joint,
            preferred_element_type=jnp.float32,
        )
        * col_scale
    ).astype(jnp.bfloat16)
    group_here = owner_ids[lax.axis_index("dp")]
    fragment = lax.all_gather(prefix_kv, "dp", axis=0, tiled=True)
    span_len = fragment.shape[0]
    match_rows = jnp.arange(span_len, dtype=jnp.int32) == group_here
    cached = jnp.sum(
        jnp.where(match_rows[:, None, None], fragment, jnp.zeros_like(fragment)), axis=0
    )
    queries = projected[:, :query_cols].reshape(row_len, heads_here, head_size).transpose(1, 0, 2)
    suffix_keys = projected[:, query_cols : query_cols + head_size]
    suffix_values = projected[:, query_cols + head_size :]
    request_ids = segment_ids[0]
    positions = jnp.arange(row_len, dtype=jnp.int32)
    allowed = (positions[None, :] <= positions[:, None]) & (
        request_ids[None, :] == request_ids[:, None]
    )
    start_state = (
        jnp.full((heads_here, row_len), -jnp.inf, jnp.float32),
        jnp.zeros((heads_here, row_len), jnp.float32),
        jnp.zeros((heads_here, row_len, head_size), jnp.float32),
    )
    suffix_state = attend_block(start_state, queries, suffix_keys, suffix_values, allowed)
    fragment = lax.all_gather(cached, "tensor", axis=0, tiled=True)
    state_out = suffix_state
    for row_begin in range(0, fragment.shape[0], 1024):
        block_rows = fragment[row_begin : row_begin + 1024]
        state_out = attend_block(
            state_out, queries, block_rows[:, :head_size], block_rows[:, head_size:], None
        )
    running, totals, weighted = state_out
    attn_heads = (
        (weighted / totals[..., None])
        .astype(jnp.bfloat16)
        .transpose(1, 0, 2)
        .reshape(row_len, query_cols)
    )
    term = jnp.dot(attn_heads, w_out, preferred_element_type=jnp.float32)
    attended = lax.psum_scatter(
        term.astype(jnp.bfloat16).astype(jnp.float32).astype(jnp.bfloat16),
        "tensor",
        scatter_dimension=0,
        tiled=True,
    )
    middle = (hidden_in.astype(jnp.float32) + attended.astype(jnp.float32)).astype(jnp.bfloat16)
    normed2 = layer_norm(middle, norm2_gain)
    hidden_act = jax.nn.gelu(
        jnp.dot(
            lax.all_gather(normed2, "tensor", axis=0, tiled=True),
            w_fc,
            preferred_element_type=jnp.float32,
        ),
        approximate=True,
    ).astype(jnp.bfloat16)
    term = jnp.dot(hidden_act, w_proj, preferred_element_type=jnp.float32)
    mlp_sum = lax.psum_scatter(
        term.astype(jnp.bfloat16).astype(jnp.float32).astype(jnp.bfloat16),
        "tensor",
        scatter_dimension=0,
        tiled=True,
    ).astype(jnp.float32)
    layer_out = (middle.astype(jnp.float32) + mlp_sum).astype(jnp.bfloat16)
    return (layer_out, attended)


def solution(mesh):
    return jax.shard_map(
        local,
        mesh=mesh,
        in_specs=(
            P(("dp", "tensor"), None),
            P(),
            P(),
            P(None, "tensor"),
            P(),
            P("tensor", None),
            P(None, "tensor"),
            P("tensor", None),
            P("dp", "tensor", None),
            P(),
            P("dp", None),
        ),
        out_specs=(P(("dp", "tensor"), None), P(("dp", "tensor"), None)),
        check_vma=False,
    )
```

profile of v0, /device:TPU:0, one launch (start us, length us, event | category | flops | bytes accessed | tf_op | source)
XLA Modules:
  0.0 392.4 jit_solution(12325680166661259745)
XLA Ops:
  8.7 1.1 convert_reduce_fusion.1
  9.8 1.3 fusion.102
  11.1 2.0 fusion.104
  13.2 1.2 dynamic_slice.3
  15.1 13.9 %all-gather.7.cloned.1.call-done = bf16[4,512,256]{2,1,0:T(8,128)(2,1)} async-done(((bf16[1,512,256]{2,1,0:T(8,128)(2,1)}), bf16[4,512,256]{2,1,0:T(8,128)(2,1)}) %all-gather.7.cloned.1.call-update) | async-done | bytes 1048592 | tf_op jit(solution)/shard_map/all_gather | solution.py:64
  29.1 2.2 select_reduce_fusion.1
  31.4 0.7 reduce.1
  32.4 59.8 %all-gather.5.cloned.1.call-done = bf16[768,2048]{1,0:T(8,128)(2,1)} async-done(((bf16[96,2048]{1,0:T(8,128)(2,1)}), bf16[768,2048]{1,0:T(8,128)(2,1)}) %all-gather.5.cloned.1.call-update) | async-done | bytes 3145744 | tf_op jit(solution)/shard_map/all_gather | solution.py:57
  92.3 4.0 %multiply_convert_fusion = bf16[768,512]{0,1:T(8,128)(2,1)S(1)} fusion(bf16[768,2048]{1,0:T(8,128)(2,1)} %all-gather.5.cloned.1.call-done, bf16[2048,256]{1,0:T(8,128)(2,1)S(1)} %copy-done.5, bf16[2048,256]{1,0:T(8,128)(2,1)} %param.14, f32[512]{0:T(512)S(1)} %copy-done.6), kind=kOutput, calls=%fused_computation.49 | convolution fusion | flops 1615593472 | bytes 6031360 | tf_op jit(solution)/shard_map/dot_general | solution.py:56
  96.6 1.0 select_reduce_fusion
  97.6 2.1 copy-done.1
  99.7 0.9 fusion.8
  100.6 42.3 %all-gather.9.cloned.1.call-done = bf16[4096,256]{1,0:T(8,128)(2,1)} async-done(((bf16[512,256]{1,0:T(8,128)(2,1)}), bf16[4096,256]{1,0:T(8,128)(2,1)}) %all-gather.9.cloned.1.call-update) | async-done | bytes 2097168 | tf_op jit(solution)/shard_map/all_gather | solution.py:84
  142.9 2.2 fusion.136
  145.1 1.1 fusion.137
  146.2 1.1 fusion.138
  147.3 1.1 fusion.135
  148.3 2.6 fusion
  150.9 2.4 fusion.4
  153.4 1.3 fusion.50
  154.7 1.3 fusion.53
  155.9 1.3 fusion.56
  157.2 1.3 fusion.59
  158.5 1.6 fusion.92
  160.1 2.7 convolution_convert_fusion.1
  162.9 72.9 %reduce-scatter.3.cloned.1.call-done = bf16[96,2048]{1,0:T(8,128)(2,1)} async-done(((bf16[768,2048]{1,0:T(8,128)(2,1)}), bf16[96,2048]{1,0:T(8,128)(2,1)}) %reduce-scatter.3.cloned.1.call-update) | async-done | bytes 393232 | tf_op jit(solution)/shard_map/reduce_scatter | solution.py:99
  235.8 1.2 convert_reduce_fusion
  237.3 1.0 fusion.101
  238.4 59.6 %all-gather.11.cloned.1.call-done = bf16[768,2048]{1,0:T(8,128)(2,1)} async-done(((bf16[96,2048]{1,0:T(8,128)(2,1)}), bf16[768,2048]{1,0:T(8,128)(2,1)}) %all-gather.11.cloned.1.call-update) | async-done | bytes 3145744 | tf_op jit(solution)/shard_map/all_gather | solution.py:109
  298.0 12.5 %convolution_convert_fusion = bf16[768,2048]{1,0:T(8,128)(2,1)} fusion(bf16[1024,2048]{1,0:T(8,128)(2,1)} %param.18, bf16[768,2048]{1,0:T(8,128)(2,1)} %all-gather.11.cloned.1.call-done, bf16[2048,1024]{1,0:T(8,128)(2,1)} %param.17), kind=kOutput, calls=%fused_computation.17 | convolution fusion | flops 6451101696 | bytes 14680064 | tf_op jit(solution)/shard_map/dot_general | solution.py:115
  310.6 73.2 %reduce-scatter.5.cloned.1.call-done = bf16[96,2048]{1,0:T(8,128)(2,1)} async-done(((bf16[768,2048]{1,0:T(8,128)(2,1)}), bf16[96,2048]{1,0:T(8,128)(2,1)}) %reduce-scatter.5.cloned.1.call-update) | async-done | bytes 393232 | tf_op jit(solution)/shard_map/reduce_scatter | solution.py:116
  383.8 1.8 fusion.106
  (43 shorter events, 3.4 us)
Async XLA Ops:
  7.2 152.9 %copy-start = (bf16[256,2048]{1,0:T(8,128)(2,1)S(1)}, bf16[256,2048]{1,0:T(8,128)(2,1)}, u32[]{:S(2)}) copy-start(bf16[256,2048]{1,0:T(8,128)(2,1)} %param.16) | copy-start | bytes 3145732
  7.2 85.1 %copy-start.6 = (f32[512]{0:T(512)S(1)}, f32[512]{0:T(512)}, u32[]{:S(2)}) copy-start(f32[512]{0:T(512)} %constant.8.clone.1) | copy-start | bytes 6148
  7.2 85.1 %copy-start.5 = (bf16[2048,256]{1,0:T(8,128)(2,1)S(1)}, bf16[2048,256]{1,0:T(8,128)(2,1)}, u32[]{:S(2)}) copy-start(bf16[2048,256]{1,0:T(8,128)(2,1)} %param.15) | copy-start | bytes 3145732
  7.2 21.9 %all-gather.7.cloned.1.call-start = ((), (), s32[]{:S(2)}) async-start(), calls=%async_computation.3 | async-start | bytes 1310720 | tf_op jit(solution)/shard_map/all_gather | solution.py:64
  7.9 84.4 %all-gather.5.cloned.1.call-start = ((), (), s32[]{:S(2)}) async-start(), calls=%async_computation.2 | async-start | bytes 3538944 | tf_op jit(solution)/shard_map/all_gather | solution.py:57
  13.2 129.8 %all-gather.9.cloned.1.call-start = ((), (), s32[]{:S(2)}) async-start(), calls=%async_computation.4 | async-start | bytes 2359296 | tf_op jit(solution)/shard_map/all_gather | solution.py:84
  31.3 204.5 %reduce-scatter.3.cloned.1.call-start = ((), (), s32[]{:S(2)}) async-start(), calls=%async_computation.5 | async-start | bytes 3538944 | tf_op jit(solution)/shard_map/reduce_scatter | solution.py:99
  97.6 2.1 copy-start.1
  142.9 2.2 copy-start.3
  154.7 3.8 slice-start
  155.9 2.5 slice-start.1
  160.1 2.8 copy-start.4
  160.1 75.7 %copy-start.2 = (bf16[96,2048]{1,0:T(8,128)(2,1)S(1)}, bf16[96,2048]{1,0:T(8,128)(2,1)}, u32[]{:S(2)}) copy-start(bf16[96,2048]{1,0:T(8,128)(2,1)} %param.11) | copy-start | bytes 1179652
  162.8 135.2 %all-gather.11.cloned.1.call-start = ((), (), s32[]{:S(2)}) async-start(), calls=%async_computation.6 | async-start | bytes 3538944 | tf_op jit(solution)/shard_map/all_gather | solution.py:109
  238.4 145.4 %reduce-scatter.5.cloned.1.call-start = ((), (), s32[]{:S(2)}) async-start(), calls=%async_computation.7 | async-start | bytes 3538944 | tf_op jit(solution)/shard_map/reduce_scatter | solution.py:116
Sparse Core Ops, SparseCore 0:
  9.6 19.4 all-gather.6
  31.8 60.4 all-gather.4
  95.0 47.9 all-gather.8
  162.9 72.8 reduce-scatter.2
  238.5 59.5 all-gather.10
  310.7 73.0 reduce-scatter.4
where the time goes:
time: 393 us; the launch traced here: 392 us
  waiting for transfers between devices  323 us (82%)
  matrix products  32.1 us (8%)
  other arithmetic  19.4 us (5%)
  between operations  14.4 us (4%)
    reduce_scatter x2, waiting for transfers between devices, local(): lax.psum_scatter(term.astype(jnp.bfloat16).astype(jnp.float32).astype(jnp...  146 us
    all_gather x1, waiting for transfers between devices, local(): lax.all_gather(normed, 'tensor', axis=0, tiled=True)  59.8 us
    all_gather x1, waiting for transfers between devices, local(): lax.all_gather(normed2, 'tensor', axis=0, tiled=True)  59.6 us
    all_gather x1, waiting for transfers between devices, local(): fragment = lax.all_gather(cached, 'tensor', axis=0, tiled=True)  42.3 us
    all_gather x1, waiting for transfers between devices, local(): fragment = lax.all_gather(prefix_kv, 'dp', axis=0, tiled=True)  13.9 us
    dot_general x1, matrix products, local(): term = jnp.dot(hidden_act, w_proj, preferred_element_type=jnp.float32)  12.5 us
  transfers between devices with their start and end apart: 6, of which 6 were waited for; matrix products, arithmetic and copies ran while one was open for 4% of the time, Pallas kernels for 0%

commit v1 on v0

--- a/solution.py
+++ b/solution.py
@@ -61,7 +61,19 @@
         * col_scale
     ).astype(jnp.bfloat16)
     group_here = owner_ids[lax.axis_index("dp")]
-    fragment = lax.all_gather(prefix_kv, "dp", axis=0, tiled=True)
+    n_lanes = lax.axis_size("dp")
+    in_order = tuple(((no, (no + 1) % n_lanes) for no in range(n_lanes)))
+    pages = tuple(((no, (no - 1) % n_lanes) for no in range(n_lanes)))
+    x_new, odd = ([prefix_kv], [prefix_kv])
+    for _ in range(n_lanes // 2):
+        x_new.append(lax.ppermute(x_new[-1], axis_name="dp", perm=in_order))
+    for _ in range((n_lanes - 1) // 2):
+        odd.append(lax.ppermute(odd[-1], axis_name="dp", perm=pages))
+    fragment = jnp.roll(
+        jnp.concatenate([*x_new[::-1], *odd[1:]], 0),
+        (lax.axis_index("dp") - n_lanes // 2) * prefix_kv.shape[0],
+        0,
+    )
     span_len = fragment.shape[0]
     match_rows = jnp.arange(span_len, dtype=jnp.int32) == group_here
     cached = jnp.sum(

time: 393 us -> 376 us (0.957)
  waiting for transfers between devices: 323 us -> 305 us
    all_gather x1 -> x0, waiting for transfers between devices: 13.9 us -> none  [local(): fragment = lax.all_gather(prefix_kv, 'dp', axis=0, tiled=True)]
    all_gather x1, waiting for transfers between devices: 59.8 us -> 46.4 us  [local(): lax.all_gather(normed, 'tensor', axis=0, tiled=True)]
    ppermute x0 -> x3, waiting for transfers between devices: none -> 11 us  [the longest x2 8.35 us: local(): x_new.append(lax.ppermute(x_new[-1], axis_name='dp', perm=in_order))]
  transfers between devices with their start and end apart: 6 -> 8, of which waited for: 6 -> 8; matrix products, arithmetic and copies ran while one was open for 4% -> 3% of each run, Pallas kernels for 0% -> 0%
where the time goes in v1:
time: 376 us
  waiting for transfers between devices  305 us (81%)
  matrix products  32.2 us (9%)
  other arithmetic  17.7 us (5%)
  between operations  14.1 us (4%)
  local copies, waits for them, and re-layouts  4.42 us (1%)
    reduce_scatter x2, waiting for transfers between devices, local(): lax.psum_scatter(term.astype(jnp.bfloat16).astype(jnp.float32).astype(jnp...  145 us
    all_gather x1, waiting for transfers between devices, local(): lax.all_gather(normed2, 'tensor', axis=0, tiled=True)  59.6 us
    all_gather x1, waiting for transfers between devices, local(): lax.all_gather(normed, 'tensor', axis=0, tiled=True)  46.4 us
    all_gather x1, waiting for transfers between devices, local(): fragment = lax.all_gather(cached, 'tensor', axis=0, tiled=True)  42.3 us
    dot_general x1, matrix products, local(): term = jnp.dot(hidden_act, w_proj, preferred_element_type=jnp.float32)  12.6 us
    ppermute x2, waiting for transfers between devices, local(): x_new.append(lax.ppermute(x_new[-1], axis_name='dp', perm=in_order))  8.35 us
  transfers between devices with their start and end apart: 8, of which 8 were waited for; matrix products, arithmetic and copies ran while one was open for 3% of the time, Pallas kernels for 0%

profile of v1, /device:TPU:0, one launch (start us, length us, event | category | flops | bytes accessed | tf_op | source)
XLA Modules:
  0.0 375.8 jit_solution(14206177625585959482)
XLA Ops:
  7.2 1.3 convert_reduce_fusion.1
  8.5 1.3 fusion.102
  10.5 2.0 fusion.104
  13.1 6.2 %collective-permute-done = bf16[1,512,256]{2,1,0:T(8,128)(2,1)S(1)} collective-permute-done((bf16[1,512,256]{2,1,0:T(8,128)(2,1)}, bf16[1,512,256]{2,1,0:T(8,128)(2,1)S(1)}, u32[]{:S(2)}, u32[]{:S(2)}) %collective-permute-start) | collective-permute-done | bytes 262176 | tf_op jit(solution)/shard_map/ppermute | solution.py:69
  19.3 1.7 collective-permute-start.2
  21.1 1.2 dynamic_slice.7
  23.0 2.1 collective-permute-done.1
  25.2 2.6 collective-permute-done.2
  28.0 1.0 select_reduce_fusion.1
  29.5 46.4 %all-gather.4.cloned.1.call-done = bf16[768,2048]{1,0:T(8,128)(2,1)} async-done(((bf16[96,2048]{1,0:T(8,128)(2,1)}), bf16[768,2048]{1,0:T(8,128)(2,1)}) %all-gather.4.cloned.1.call-update) | async-done | bytes 3145744 | tf_op jit(solution)/shard_map/all_gather | solution.py:57
  75.8 4.0 %multiply_convert_fusion = bf16[768,512]{0,1:T(8,128)(2,1)S(1)} fusion(bf16[768,2048]{1,0:T(8,128)(2,1)} %all-gather.4.cloned.1.call-done, bf16[2048,256]{1,0:T(8,128)(2,1)S(1)} %copy-done.8, bf16[2048,256]{1,0:T(8,128)(2,1)} %param.14, f32[512]{0:T(512)S(1)} %copy-done.9), kind=kOutput, calls=%fused_computation.49 | convolution fusion | flops 1615593472 | bytes 6031360 | tf_op jit(solution)/shard_map/dot_general | solution.py:56
  81.1 2.1 copy-done.2
  84.2 42.3 %all-gather.6.cloned.1.call-done = bf16[4096,256]{1,0:T(8,128)(2,1)} async-done(((bf16[512,256]{1,0:T(8,128)(2,1)}), bf16[4096,256]{1,0:T(8,128)(2,1)}) %all-gather.6.cloned.1.call-update) | async-done | bytes 2097168 | tf_op jit(solution)/shard_map/all_gather | solution.py:96
  126.5 2.2 fusion.136
  128.6 1.1 fusion.137
  129.7 1.1 fusion.138
  130.8 1.1 fusion.135
  131.9 2.7 fusion
  134.6 2.4 fusion.4
  137.0 1.3 fusion.50
  138.3 1.3 fusion.53
  139.6 1.3 fusion.56
  140.9 1.3 fusion.59
  142.1 1.6 fusion.92
  143.7 2.7 convolution_convert_fusion.1
  147.1 72.4 %reduce-scatter.3.cloned.1.call-done = bf16[96,2048]{1,0:T(8,128)(2,1)} async-done(((bf16[768,2048]{1,0:T(8,128)(2,1)}), bf16[96,2048]{1,0:T(8,128)(2,1)}) %reduce-scatter.3.cloned.1.call-update) | async-done | bytes 393232 | tf_op jit(solution)/shard_map/reduce_scatter | solution.py:111
  219.5 1.2 convert_reduce_fusion
  221.0 1.0 fusion.101
  222.1 59.6 %all-gather.8.cloned.1.call-done = bf16[768,2048]{1,0:T(8,128)(2,1)} async-done(((bf16[96,2048]{1,0:T(8,128)(2,1)}), bf16[768,2048]{1,0:T(8,128)(2,1)}) %all-gather.8.cloned.1.call-update) | async-done | bytes 3145744 | tf_op jit(solution)/shard_map/all_gather | solution.py:121
  281.7 12.6 %convolution_convert_fusion = bf16[768,2048]{1,0:T(8,128)(2,1)} fusion(bf16[1024,2048]{1,0:T(8,128)(2,1)} %param.18, bf16[768,2048]{1,0:T(8,128)(2,1)} %all-gather.8.cloned.1.call-done, bf16[2048,1024]{1,0:T(8,128)(2,1)} %param.17), kind=kOutput, calls=%fused_computation.17 | convolution fusion | flops 6451101696 | bytes 14680064 | tf_op jit(solution)/shard_map/dot_general | solution.py:127
  294.3 73.1 %reduce-scatter.5.cloned.1.call-done = bf16[96,2048]{1,0:T(8,128)(2,1)} async-done(((bf16[768,2048]{1,0:T(8,128)(2,1)}), bf16[96,2048]{1,0:T(8,128)(2,1)}) %reduce-scatter.5.cloned.1.call-update) | async-done | bytes 393232 | tf_op jit(solution)/shard_map/reduce_scatter | solution.py:128
  367.4 1.8 fusion.106
  (60 shorter events, 5.9 us)
Async XLA Ops:
  7.2 136.6 %copy-start = (bf16[256,2048]{1,0:T(8,128)(2,1)S(1)}, bf16[256,2048]{1,0:T(8,128)(2,1)}, u32[]{:S(2)}) copy-start(bf16[256,2048]{1,0:T(8,128)(2,1)} %param.16) | copy-start | bytes 3145732
  7.2 18.0 %copy-start.5 = (bf16[1,512,256]{2,1,0:T(8,128)(2,1)S(1)}, bf16[1,512,256]{2,1,0:T(8,128)(2,1)}, u32[]{:S(2)}) copy-start(bf16[1,512,256]{2,1,0:T(8,128)(2,1)} %param.19) | copy-start | bytes 786436
  7.2 68.6 %all-gather.4.cloned.1.call-start = ((), (), s32[]{:S(2)}) async-start(), calls=%async_computation.2 | async-start | bytes 3538944 | tf_op jit(solution)/shard_map/all_gather | solution.py:57
  12.5 16.6 %copy-start.7 = (s32[1,768]{1,0:T(1,128)S(1)}, s32[1,768]{1,0:T(1,128)}, u32[]{:S(2)}) copy-start(s32[1,768]{1,0:T(1,128)} %param.21) | copy-start | bytes 9220
  12.5 113.9 %all-gather.6.cloned.1.call-start = ((), (), s32[]{:S(2)}) async-start(), calls=%async_computation.3 | async-start | bytes 2359296 | tf_op jit(solution)/shard_map/all_gather | solution.py:96
  12.6 6.7 %collective-permute-start = (bf16[1,512,256]{2,1,0:T(8,128)(2,1)}, bf16[1,512,256]{2,1,0:T(8,128)(2,1)S(1)}, u32[]{:S(2)}, u32[]{:S(2)}) collective-permute-start(bf16[1,512,256]{2,1,0:T(8,128)(2,1)} %param.19), channel_id=1, source_target_pairs={{0,8},{8,16},{16,24},{24,0},{1,9},{9,17},{17,25},{25,1},{2,10},{10... | collective-permute-start | bytes 786440 | tf_op jit(solution)/shard_map/ppermute | solution.py:69
  19.3 5.8 %collective-permute-start.1 = (bf16[1,512,256]{2,1,0:T(8,128)(2,1)S(1)}, bf16[1,512,256]{2,1,0:T(8,128)(2,1)S(1)}, u32[]{:S(2)}, u32[]{:S(2)}) collective-permute-start(bf16[1,512,256]{2,1,0:T(8,128)(2,1)S(1)} %collective-permute-done), channel_id=1, source_target_pairs={{0,8},{8,16},{16,24},{24,0},{1,9},{9,17},{17,25},{25,1},{2,10},{10... | collective-permute-start | bytes 786440 | tf_op jit(solution)/shard_map/ppermute | solution.py:69
  19.3 8.5 %collective-permute-start.2 = (bf16[1,512,256]{2,1,0:T(8,128)(2,1)}, bf16[1,512,256]{2,1,0:T(8,128)(2,1)S(1)}, u32[]{:S(2)}, u32[]{:S(2)}) collective-permute-start(bf16[1,512,256]{2,1,0:T(8,128)(2,1)} %param.19), channel_id=1, source_target_pairs={{0,24},{8,0},{16,8},{24,16},{1,25},{9,1},{17,9},{25,17},{2,26},{10... | collective-permute-start | bytes 786440 | tf_op jit(solution)/shard_map/ppermute | solution.py:71
  23.0 52.9 %copy-start.8 = (bf16[2048,256]{1,0:T(8,128)(2,1)S(1)}, bf16[2048,256]{1,0:T(8,128)(2,1)}, u32[]{:S(2)}) copy-start(bf16[2048,256]{1,0:T(8,128)(2,1)} %param.15) | copy-start | bytes 3145732
  23.0 52.9 %copy-start.9 = (f32[512]{0:T(512)S(1)}, f32[512]{0:T(512)}, u32[]{:S(2)}) copy-start(f32[512]{0:T(512)} %constant.49.clone.1) | copy-start | bytes 6148
  29.0 190.5 %reduce-scatter.3.cloned.1.call-start = ((), (), s32[]{:S(2)}) async-start(), calls=%async_computation.4 | async-start | bytes 3538944 | tf_op jit(solution)/shard_map/reduce_scatter | solution.py:111
  81.1 2.1 copy-start.2
  126.5 2.2 copy-start.4
  138.3 3.8 %slice-start = ((s8[4718592]{0:T(1024)(128)(4,1)}), s8[524288]{0:T(1024)(128)(4,1)S(1)}, s32[]{:S(2)}) async-start(s8[4718592]{0:T(1024)(128)(4,1)} %bitcast.196), calls=%async_computation.7 | async-start | bytes 1048576
  139.6 2.5 slice-start.1
  146.4 0.7 copy-start.6
  146.4 73.1 %copy-start.3 = (bf16[96,2048]{1,0:T(8,128)(2,1)S(1)}, bf16[96,2048]{1,0:T(8,128)(2,1)}, u32[]{:S(2)}) copy-start(bf16[96,2048]{1,0:T(8,128)(2,1)} %param.11) | copy-start | bytes 1179652
  146.4 135.3 %all-gather.8.cloned.1.call-start = ((), (), s32[]{:S(2)}) async-start(), calls=%async_computation.5 | async-start | bytes 3538944 | tf_op jit(solution)/shard_map/all_gather | solution.py:121
  222.1 145.3 %reduce-scatter.5.cloned.1.call-start = ((), (), s32[]{:S(2)}) async-start(), calls=%async_computation.6 | async-start | bytes 3538944 | tf_op jit(solution)/shard_map/reduce_scatter | solution.py:128
  281.7 87.5 %copy-start.1 = (bf16[256,2048]{1,0:T(8,128)(2,1)S(1)}, bf16[256,2048]{1,0:T(8,128)(2,1)}, u32[]{:S(2)}) copy-start(bf16[256,2048]{1,0:T(8,128)(2,1)} %param.16) | copy-start | bytes 3145732
Sparse Core Ops, SparseCore 0:
  12.7 63.1 all-gather.3
  78.5 47.9 all-gather.5
  146.6 72.8 reduce-scatter.2
  222.2 59.5 all-gather.7
  294.4 72.8 reduce-scatter.4
